TPU v7x, 32 devices: a whole 2x2x4 slice. The times are simulated.
32 devices in a mesh: beam: 8 (over z, y), elem: 4 (over x, core).
Axes of the slice: x: 2, y: 2, z: 4, core: 2. Of those that a mesh axis runs over, the one named last changes fastest.
Arguments:
- signals: bfloat16 [2, 16384, 256], P(None, 'elem', 'beam'), may hold values from -6 to 6
- weights: bfloat16 [2, 16384, 16384], P(None, 'beam', 'elem'), may hold values from -0.0625 to 0.0625
- element_flags: int32 [16384], P('elem'), may hold values from 0 to 1, as said below
Outputs:
- beam_out: bfloat16 [2, 16384, 256], P(None, ('beam', 'elem'))
- beam_power: float32 [16384], P(('beam', 'elem'))
Inputs may be any that keep to these rules, and one draw needn't show every extreme that they name: `element_flags`: element 16384 - 1 is always live.
All inputs are finite; a program needn't handle non-finite values.
Results may differ from a plain program's by a relative error of at most 0.001.
Values may be sent and summed in bfloat16 or wider, within the bound.
A program may use at most 128 MiB of HBM per device.

v0:
```python
import jax
import jax.numpy as jnp
from jax import lax
from jax.sharding import PartitionSpec as P

E = 16384


def body(signals, weights, element_flags):
    masked = signals * element_flags.astype(jnp.bfloat16)[None, :, None]
    live_total = lax.psum(jnp.sum(element_flags.astype(jnp.float32)), "elem")
    beam_gain = jnp.sqrt(jnp.float32(E) / live_total)
    gathered = lax.all_gather(masked, "beam", axis=2, tiled=True)
    snap_count = gathered.shape[2]
    upper_half = jnp.concatenate([gathered[0], gathered[1]], axis=1)
    lower_half = jnp.concatenate([-gathered[1], gathered[0]], axis=1)
    stacked = jnp.concatenate([upper_half, lower_half], axis=0)
    joined = jnp.concatenate([weights[0], weights[1]], axis=1)
    own_rows = lax.psum_scatter(
        jnp.dot(joined, stacked, preferred_element_type=jnp.float32),
        "elem",
        scatter_dimension=0,
        tiled=True,
    )
    received = jnp.stack([own_rows[:, :snap_count], own_rows[:, snap_count:]])
    scaled = received * beam_gain
    beam_out = scaled.astype(jnp.bfloat16)
    beam_power = jnp.mean(scaled[0] * scaled[0] + scaled[1] * scaled[1], axis=1)
    return (beam_out, beam_power)


def solution(mesh):
    return jax.shard_map(
        body,
        mesh=mesh,
        in_specs=(P(None, "elem", "beam"), P(None, "beam", "elem"), P("elem")),
        out_specs=(P(None, ("beam", "elem"), None), P(("beam", "elem"))),
        check_vma=False,
    )
```

profile of v0, /device:TPU:0, one launch (start us, length us, event | category | flops | bytes accessed | tf_op | source)
XLA Modules:
  0.0 176.8 jit_solution(3727435873431027975)
XLA Ops:
  7.2 0.0 all-gather.2.cloned.1.call-start
  7.2 0.7 convert_element_type.9
  7.9 1.9 %broadcast_multiply_fusion = bf16[2,4096,32]{1,2,0:T(8,128)(2,1)} fusion(bf16[2,4096,32]{1,2,0:T(8,128)(2,1)} %param.3, bf16[4096]{0:T(1024)(128)(2,1)S(1)} %convert_element_type.9), kind=kLoop, calls=%fused_computation.22 | loop fusion | flops 262144 | bytes 1056768 | tf_op jit(solution)/shard_map/mul | solution.py:10
  9.8 0.0 all-gather.2.cloned.1.call-update
  9.8 0.0 reduce-scatter.2.cloned.1.call-start
  9.9 23.3 %slice_bitcast_fusion.1 = (bf16[2048,4096]{1,0:T(8,128)(2,1)}, bf16[2048,4096]{1,0:T(8,128)(2,1)}) fusion(bf16[2,2048,4096]{2,1,0:T(8,128)(2,1)} %param.4), kind=kLoop, calls=%fused_computation.5 | loop fusion | bytes 67108864 | tf_op jit(solution)/shard_map/squeeze | solution.py:18
  33.2 53.0 %all-gather.2.cloned.1.call-done = bf16[2,4096,256]{1,2,0:T(8,128)(2,1)} async-done(((bf16[2,4096,32]{1,2,0:T(8,128)(2,1)}), bf16[2,4096,256]{1,2,0:T(8,128)(2,1)}) %all-gather.2.cloned.1.call-update) | async-done | bytes 4194320 | tf_op jit(solution)/shard_map/all_gather | solution.py:13
  86.3 4.7 %slice_bitcast_fusion.2 = (bf16[4096,256]{0,1:T(8,128)(2,1)}, bf16[4096,256]{0,1:T(8,128)(2,1)}) fusion(bf16[2,4096,256]{1,2,0:T(8,128)(2,1)} %all-gather.2.cloned.1.call-done), kind=kLoop, calls=%fused_computation.13 | loop fusion | bytes 8388608 | tf_op jit(solution)/shard_map/squeeze | solution.py:15
  90.9 1.7 fusion.14
  92.7 0.0 copy-start
  92.7 31.1 %fusion = f32[2048,512]{1,0:T(8,128)} fusion(bf16[2048,4096]{1,0:T(8,128)(2,1)} %get-tuple-element.5, bf16[2048,4096]{1,0:T(8,128)(2,1)} %get-tuple-element.4, bf16[4096,256]{0,1:T(8,128)(2,1)} %get-tuple-element.7, bf16[4096,256]{0,1:T(8,128)(2,1)S(1)} %fusion.14, bf16[4096,256]{0,1:T(8,128)(2,1)} %get-tuple-element.6), kind=kOutput, calls=%fused_computation | convolution fusion | flops 17280532480 | bytes 44040192 | tf_op jit(solution)/shard_map/dot_general | solution.py:20
  123.8 0.0 reduce-scatter.2.cloned.1.call-update
  123.8 0.0 copy-done
  123.8 0.6 convert_reduce_fusion
  124.4 6.3 %psum.7 = f32[]{:T(128)} all-reduce(f32[]{:T(128)} %convert_reduce_fusion), channel_id=1, replica_groups=mesh['beam'=8,'elem'=4] {'elem'}, use_global_device_ids=true, to_apply=%region_2.0 | all-reduce | flops 1 | bytes 8 | tf_op jit(solution)/shard_map/psum | solution.py:11
  131.4 35.6 %reduce-scatter.2.cloned.1.call-done = f32[512,512]{1,0:T(8,128)} async-done(((f32[2048,512]{1,0:T(8,128)}), f32[512,512]{1,0:T(8,128)}) %reduce-scatter.2.cloned.1.call-update) | async-done | bytes 1048592 | tf_op jit(solution)/shard_map/reduce_scatter | solution.py:19
  167.1 1.3 slice_bitcast_fusion.5
  168.4 0.9 fusion.15
  169.3 0.1 fusion.12
  169.4 0.6 broadcast_multiply_fusion.1
Async XLA Ops:
  7.2 79.1 %all-gather.2.cloned.1.call-start = ((), (), s32[]{:S(2)}) async-start(), calls=%async_computation.1 | async-start | bytes 4718592 | tf_op jit(solution)/shard_map/all_gather | solution.py:13
  9.8 157.3 %reduce-scatter.2.cloned.1.call-start = ((), (), s32[]{:S(2)}) async-start(), calls=%async_computation.2 | async-start | bytes 5242880 | tf_op jit(solution)/shard_map/reduce_scatter | solution.py:19
  92.7 31.2 %copy-start = (s32[4096]{0:T(1024)S(1)}, s32[4096]{0:T(1024)}, u32[]{:S(2)}) copy-start(s32[4096]{0:T(1024)} %param.5) | copy-start | bytes 49156
Sparse Core Ops, SparseCore 0:
  10.7 75.4 all-gather.1
  123.9 43.1 reduce-scatter.1
where the time goes:
time: 177 us
  waiting for transfers between devices  88.7 us (50%)
  matrix products  31.1 us (18%)
  local copies, waits for them, and re-layouts  29.3 us (17%)
  between operations  14.8 us (8%)
  other arithmetic  6.57 us (4%)
  blocking collectives  6.27 us (4%)
    all_gather x1, waiting for transfers between devices, body(): gathered = lax.all_gather(masked, 'beam', axis=2, tiled=True)  53 us
    reduce_scatter x1, waiting for transfers between devices, body(): lax.psum_scatter(jnp.dot(joined, stacked, preferred_element_type=jnp.floa...  35.6 us
    dot_general x1, matrix products, body(): jnp.dot(joined, stacked, preferred_element_type=jnp.float32)  31.1 us
    squeeze x1, local copies, waits for them, and re-layouts, body(): joined = jnp.concatenate([weights[0], weights[1]], axis=1)  23.3 us
    psum x1, blocking collectives, body(): live_total = lax.psum(jnp.sum(element_flags.astype(jnp.float32)), 'elem')  6.27 us
    squeeze x1, local copies, waits for them, and re-layouts, body(): upper_half = jnp.concatenate([gathered[0], gathered[1]], axis=1)  4.66 us
  transfers between devices with their start and end apart: 2, of which 2 were waited for; matrix products, arithmetic and copies ran while one was open for 14% of the time, Pallas kernels for 0%

commit v1 on v0

v1 whole, which is shorter than its diff:
```python
import functools

import jax
import jax.numpy as jnp
from jax import lax
from jax.experimental import pallas as pl
from jax.experimental.pallas import tpu as pltpu
from jax.sharding import PartitionSpec as P

PIECES = 4
LANES = 128
MESH = pl.DeviceIdType.MESH


def ring_order(mesh):
    nb = mesh.shape["beam"]
    try:
        coords = [tuple(d.coords) for d in mesh.devices[:, 0]]
    except AttributeError:
        return list(range(nb))
    axes = [a for a in range(len(coords[0])) if len({c[a] for c in coords}) > 1]
    if len(axes) != 2:
        return list(range(nb))
    values = [sorted({c[a] for c in coords}) for a in axes]
    if len(values[0]) % 2:
        axes, values = axes[::-1], values[::-1]
    rows, cols = len(values[0]), len(values[1])
    if rows % 2 or rows * cols != nb:
        return list(range(nb))
    at = {(values[0].index(c[axes[0]]), values[1].index(c[axes[1]])): i for i, c in enumerate(coords)}
    path = [(0, 0)]
    for r in range(rows):
        inner = range(1, cols) if r % 2 == 0 else range(cols - 1, 0, -1)
        path += [(r, c) for c in inner]
    path += [(r, 0) for r in range(rows - 1, 0, -1)]
    return [at[p] for p in path]


def lookup(table, index):
    value = jnp.int32(table[0])
    for i in range(1, len(table)):
        value = jnp.where(index == i, jnp.int32(table[i]), value)
    return value


def kernel(order, ne, elements, s_ref, cnt_ref, w_ref, out_ref, pow_ref,
           blocks, weights, rhs, part, first, second, counts,
           ring_send, ring_recv, w_sem, s_sem, first_send, first_recv, second_send, second_recv,
           cnt_send, cnt_recv, cnt_sem):
    nb = len(order)
    half = nb // 2
    q, two_t, kq = s_ref.shape
    tb = two_t // 2
    chunks, _, mo, width = part.shape
    group = width // two_t
    ways = ne // 2
    snaps = nb * tb

    me_b = lax.axis_index("beam")
    me_e = lax.axis_index("elem")
    inverse = [order.index(i) for i in range(nb)]
    pos = lookup(inverse, me_b)
    ahead = lookup([order[(inverse[i] + 1) % nb] for i in range(nb)], me_b)
    behind = lookup([order[(inverse[i] - 1) % nb] for i in range(nb)], me_b)
    core = lax.rem(me_e, 2)
    mine = me_e // 2
    partner = me_e + 1 - 2 * core

    def slot_of(way, d):
        return d if (way == 0 or d in (0, half)) else half + d

    arrivals = [[(d, j) for d in range(1, half) for j in range(q)]
                + [(half, j) for j in (range(q // 2) if way == 0 else range(q // 2, q))]
                for way in (0, 1)]
    number = [{item: k for k, item in enumerate(a)} for a in arrivals]

    def ring_copy(way, d, j):
        k = number[way][(d, j)]
        return pltpu.make_async_remote_copy(
            src_ref=blocks.at[slot_of(way, d - 1), j],
            dst_ref=blocks.at[slot_of(way, d), j],
            send_sem=ring_send.at[way, k], recv_sem=ring_recv.at[way, k],
            device_id={"beam": ahead if way == 0 else behind}, device_id_type=MESH)

    def weight_copy(i, j):
        return pltpu.make_async_copy(
            w_ref.at[i, :, pl.ds(j * kq, kq)], weights.at[j, :, pl.ds(i * kq, kq)], w_sem.at[i, j])

    def count_copy(r):
        return pltpu.make_async_remote_copy(
            src_ref=cnt_ref, dst_ref=counts.at[r], send_sem=cnt_send.at[r - 1], recv_sem=cnt_recv.at[r - 1],
            device_id={"elem": lax.rem(me_e + r, ne)}, device_id_type=MESH)

    def kept(i):
        return 2 * lax.rem(mine + i, ways) + core

    def given(i):
        return 2 * lax.rem(mine + i, ways) + 1 - core

    def first_copy(c, i):
        return pltpu.make_async_remote_copy(
            src_ref=part.at[c, given(i)], dst_ref=first.at[c, i],
            send_sem=first_send.at[c, i], recv_sem=first_recv.at[c, i],
            device_id={"elem": partner}, device_id_type=MESH)

    def second_copy(c, i):
        return pltpu.make_async_remote_copy(
            src_ref=first.at[c, i], dst_ref=second.at[c, i - 1],
            send_sem=second_send.at[c, i - 1], recv_sem=second_recv.at[c, i - 1],
            device_id={"elem": kept(i)}, device_id_type=MESH)

    own_in = pltpu.make_async_copy(s_ref, blocks.at[0], s_sem)
    own_in.start()
    own_cnt = pltpu.make_async_copy(cnt_ref, counts.at[0], cnt_sem)
    own_cnt.start()

    barrier = pltpu.get_barrier_semaphore()
    for b in (ahead, behind):
        pl.semaphore_signal(barrier, inc=1, device_id={"beam": b}, device_id_type=MESH)
    for r in range(1, ne):
        pl.semaphore_signal(barrier, inc=1, device_id={"elem": lax.rem(me_e + r, ne)}, device_id_type=MESH)
    pl.semaphore_wait(barrier, 2 + ne - 1)

    own_in.wait()
    for j in range(q):
        for way in (0, 1):
            if (1, j) in number[way]:
                ring_copy(way, 1, j).start()
    for r in range(1, ne):
        count_copy(r).start()
    for j in range(q):
        for i in (0, 1):
            weight_copy(i, j).start()

    sequence = [(0, 0)]
    for d in range(1, half):
        sequence += [(0, d), (1, d)]
    sequence += [(0, half)]

    def members(c):
        return sequence[c * group:(c + 1) * group]

    def stage(c, j):
        for s, (way, d) in enumerate(members(c)):
            re = blocks[slot_of(way, d), j, :tb, :]
            im = blocks[slot_of(way, d), j, tb:, :]
            lo, hi = s * tb, (group + s) * tb
            rhs[lo:lo + tb, :kq] = re
            rhs[hi:hi + tb, :kq] = im
            rhs[lo:lo + tb, kq:] = -im
            rhs[hi:hi + tb, kq:] = re

    def multiply(c, j, o, fresh):
        rows = pl.ds(pl.multiple_of(o * mo, mo), mo)
        product = lax.dot_general(weights[j, rows, :], rhs[...], (((1,), (1,)), ((), ())),
                                  preferred_element_type=jnp.float32)
        if fresh:
            part[c, o] = product
        else:
            part[c, o] += product

    pieces_done = [0] * chunks
    weights_here = set()
    waiting = []

    def pass_on(c):
        for i in range(1, ways):
            first_copy(c, i).wait_recv()
            first[c, i] += part[c, kept(i)]
            second_copy(c, i).start()

    def piece(c, j):
        stage(c, j)
        if j not in weights_here:
            weights_here.add(j)
            for i in (0, 1):
                weight_copy(i, j).wait()
        fresh = pieces_done[c] == 0
        pieces_done[c] += 1
        if pieces_done[c] < q:
            @pl.loop(0, ne)
            def _(o):
                multiply(c, j, o, fresh)
            return
        for i in list(range(1, ways)) + [0]:
            multiply(c, j, given(i), fresh)
            first_copy(c, i).start()
        for i in range(1, ways):
            multiply(c, j, kept(i), fresh)
            if c == chunks - 1:
                first_copy(c, i).wait_recv()
                first[c, i] += part[c, kept(i)]
                second_copy(c, i).start()
        multiply(c, j, kept(0), fresh)
        if c < chunks - 1:
            waiting.append(c)

    arrived = {((0, 0), j) for j in range(q)}
    todo = [(c, j) for c in range(chunks) for j in range(q)]

    def run_ready():
        for c, j in list(todo):
            if all((m, j) in arrived for m in members(c)):
                todo.remove((c, j))
                piece(c, j)

    for k in range(len(arrivals[0])):
        for way in (0, 1):
            d, j = arrivals[way][k]
            ring_copy(way, d, j).wait_recv()
            if (d + 1, j) in number[way]:
                ring_copy(way, d + 1, j).start()
            arrived.add(((0 if d == half else way, d), j))
        for c in waiting:
            pass_on(c)
        waiting.clear()
        run_ready()
    for c in waiting:
        pass_on(c)
    waiting.clear()

    own_cnt.wait()
    total = counts[0]
    for r in range(1, ne):
        count_copy(r).wait()
        total = total + counts[r]
    gain = jnp.sqrt(jnp.float32(elements) / total)[0:1, 0:1]

    square = jnp.zeros((mo, width), jnp.float32)
    moved = jnp.zeros((mo, 2 * snaps), jnp.float32)
    for c in range(chunks):
        first_copy(c, 0).wait_recv()
        value = part[c, me_e] + first[c, 0]
        for i in range(1, ways):
            second_copy(c, i).wait_recv()
            value = value + second[c, i - 1]
        value = value * gain
        square = square + value * value
        column = lax.broadcasted_iota(jnp.int32, (width, 2 * snaps), 0)
        target = lax.broadcasted_iota(jnp.int32, (width, 2 * snaps), 1)
        wanted = column
        for s, (way, d) in enumerate(members(c)):
            source = lookup(order, lax.rem(pos + (d if way else nb - d), nb))
            for p in (0, 1):
                lo = (p * group + s) * tb
                inside = (column >= lo) & (column < lo + tb)
                wanted = jnp.where(inside, column - lo + p * snaps + source * tb, wanted)
        select = jnp.where(wanted == target, 1.0, 0.0).astype(jnp.bfloat16)
        moved = moved + jnp.dot(value.astype(jnp.bfloat16), select, preferred_element_type=jnp.float32)
    moved = moved.astype(jnp.bfloat16)
    out_ref[0] = moved[:, :snaps]
    out_ref[1] = moved[:, snaps:]
    power = jnp.sum(square, axis=1, keepdims=True) * (1.0 / snaps)
    pow_ref[...] = jnp.broadcast_to(power, pow_ref.shape)

    for way in (0, 1):
        for d, j in arrivals[way]:
            ring_copy(way, d, j).wait_send()
    for c in range(chunks):
        for i in range(ways):
            first_copy(c, i).wait_send()
        for i in range(1, ways):
            second_copy(c, i).wait_send()


def body(order, ne, signals, weights, element_flags):
    nb = len(order)
    _, depth, tb = signals.shape
    rows = weights.shape[1]
    mo = rows // ne
    q = PIECES
    kq = depth // q
    group = min(nb, max(1, LANES // tb))
    chunks = nb // group
    width = 2 * group * tb
    ways = ne // 2
    items = q * (nb // 2) - q // 2
    masked = signals * element_flags.astype(jnp.bfloat16)[None, :, None]
    sent = masked.reshape(2, q, kq, tb).transpose(1, 0, 3, 2).reshape(q, 2 * tb, kq)
    count = jnp.broadcast_to(jnp.sum(element_flags.astype(jnp.float32)), (8, LANES))
    dma = pltpu.SemaphoreType.DMA
    anywhere = pl.BlockSpec(memory_space=pl.ANY)
    vmem = pl.BlockSpec(memory_space=pltpu.VMEM)
    out, power = pl.pallas_call(
        functools.partial(kernel, order, ne, depth * ne),
        out_shape=(jax.ShapeDtypeStruct((2, mo, nb * tb), jnp.bfloat16),
                   jax.ShapeDtypeStruct((mo, LANES), jnp.float32)),
        in_specs=[anywhere, anywhere, anywhere],
        out_specs=(vmem, vmem),
        scratch_shapes=[
            pltpu.VMEM((nb, q, 2 * tb, kq), jnp.bfloat16),
            pltpu.VMEM((q, rows, 2 * kq), jnp.bfloat16),
            pltpu.VMEM((width, 2 * kq), jnp.bfloat16),
            pltpu.VMEM((chunks, ne, mo, width), jnp.float32),
            pltpu.VMEM((chunks, ways, mo, width), jnp.float32),
            pltpu.VMEM((chunks, max(1, ways - 1), mo, width), jnp.float32),
            pltpu.VMEM((ne, 8, LANES), jnp.float32),
            dma((2, items)), dma((2, items)), dma((2, q)), dma,
            dma((chunks, ways)), dma((chunks, ways)),
            dma((chunks, max(1, ways - 1))), dma((chunks, max(1, ways - 1))),
            dma((ne - 1,)), dma((ne - 1,)), dma,
        ],
        compiler_params=pltpu.CompilerParams(
            collective_id=0, has_side_effects=True, vmem_limit_bytes=60 * 2**20),
        name="beamform",
    )(sent, count, weights)
    return out, power[:, 0]


def solution(mesh):
    return jax.shard_map(
        functools.partial(body, ring_order(mesh), mesh.shape["elem"]),
        mesh=mesh,
        in_specs=(P(None, "elem", "beam"), P(None, "beam", "elem"), P("elem")),
        out_specs=(P(None, ("beam", "elem"), None), P(("beam", "elem"))),
        check_vma=False,
    )
```

time: 177 us -> 80.8 us (0.46)
  waiting for transfers between devices: 88.7 us -> 0 us
  Pallas kernels: 0 us -> 71 us
  matrix products: 31.1 us -> 0 us
  local copies, waits for them, and re-layouts: 29.3 us -> 5.61 us
  between operations: 14.8 us -> 0.64 us
  blocking collectives: 6.27 us -> 0 us
  other arithmetic: 6.57 us -> 3.13 us
    pallas_call x0 -> x1, Pallas kernels: none -> 71 us  [body(): pl.pallas_call(functools.partial(kernel, order, ne, depth * ne), out_shap...]
    all_gather x1 -> x0, waiting for transfers between devices: 53 us -> none  [body(): gathered = lax.all_gather(masked, 'beam', axis=2, tiled=True)]
    reduce_scatter x1 -> x0, waiting for transfers between devices: 35.6 us -> none  [body(): lax.psum_scatter(jnp.dot(joined, stacked, preferred_element_type=jnp.floa...]
    dot_general x1 -> x0, matrix products: 31.1 us -> none  [body(): jnp.dot(joined, stacked, preferred_element_type=jnp.float32)]
    squeeze x2 -> x0, local copies, waits for them, and re-layouts: 28 us -> none  [the longest x1 23.3 us: body(): joined = jnp.concatenate([weights[0], weights[1]], axis=1)]
    psum x1 -> x0, blocking collectives: 6.27 us -> none  [body(): live_total = lax.psum(jnp.sum(element_flags.astype(jnp.float32)), 'elem')]
    unnamed x2 -> x1, local copies, waits for them, and re-layouts: 0.01 us -> 1.87 us
  transfers between devices with their start and end apart: 2 -> 0, of which waited for: 2 -> 0; matrix products, arithmetic and copies ran while one was open for 14% -> 0% of each run, Pallas kernels for 0% -> 0%
where the time goes in v1:
time: 80.8 us; the launch traced here: 80.4 us
  Pallas kernels  71 us (88%)
  local copies, waits for them, and re-layouts  5.61 us (7%)
  other arithmetic  3.13 us (4%)
    pallas_call x1, Pallas kernels, body(): pl.pallas_call(functools.partial(kernel, order, ne, depth * ne), out_shap...  71 us
    unnamed x1, local copies, waits for them, and re-layouts  1.87 us
    slice x1, local copies, waits for them, and re-layouts, body(): return (out, power[:, 0])  1.68 us

profile of v1, /device:TPU:0, one launch (start us, length us, event | category | flops | bytes accessed | tf_op | source)
XLA Modules:
  0.0 80.4 jit_solution(5003571069254864240)
XLA Ops:
  0.6 1.3 %convert_reduce_fusion = f32[]{:T(128)} fusion(s32[4096]{0:T(1024)} %param.5), kind=kLoop, calls=%fused_computation.3 | loop fusion | flops 8191 | bytes 16388 | tf_op jit(solution)/shard_map/reduce_sum | solution.py:280
  2.0 1.2 %broadcast_in_dim.4.cnt_ref = f32[8,128]{1,0:T(8,128)} broadcast(f32[]{:T(128)} %convert_reduce_fusion), dimensions={} | broadcast | bytes 4100 | tf_op jit(solution)/shard_map/broadcast_in_dim | solution.py:280
  3.2 0.7 convert_element_type.6
  3.9 1.1 %broadcast_multiply_fusion = bf16[2,4096,32]{1,2,0:T(8,128)(2,1)S(1)} fusion(bf16[2,4096,32]{1,2,0:T(8,128)(2,1)} %param.3, bf16[4096]{0:T(1024)(128)(2,1)S(1)} %convert_element_type.6), kind=kLoop, calls=%fused_computation.2 | loop fusion | flops 262144 | bytes 1056768 | tf_op jit(solution)/shard_map/mul | solution.py:278
  5.0 0.8 %copy.9 = bf16[2,4,4,8,1024]{4,3,1,0,2:T(8,128)(2,1)} copy(bf16[2,4,4,8,1024]{4,3,2,1,0:T(8,128)(2,1)S(1)} %bitcast.8) | data formatting | bytes 1048576 | tf_op jit(solution)/shard_map/reshape | solution.py:279
  5.8 71.0 %beamform.1 = (bf16[2,512,256]{2,1,0:T(8,128)(2,1)}, f32[512,128]{1,0:T(8,128)}) custom-call(bf16[4,64,1024]{2,1,0:T(8,128)(2,1)} %bitcast.7, f32[8,128]{1,0:T(8,128)} %broadcast_in_dim.4.cnt_ref, bf16[2,2048,4096]{2,1,0:T(8,128)(2,1)} %w_ref.1), custom_call_target="tpu_custom_call" | custom-call | tf_op jit(solution)/shard_map/beamform/pallas_call | solution.py:284
  76.8 1.7 %slice_reduce_fusion = f32[512]{0:T(512)} fusion(f32[512,128]{1,0:T(8,128)} %get-tuple-element.5), kind=kLoop, calls=%fused_computation.1 | loop fusion | bytes 4096 | tf_op jit(solution)/shard_map/slice | solution.py:307
  78.5 1.9 %copy.11 = bf16[2,512,256]{2,1,0:T(8,128)(2,1)} copy(bf16[2,512,256]{2,1,0:T(8,128)(2,1)} %get-tuple-element.8) | data formatting | bytes 1048576

commit v2 on v1

--- a/solution.py
+++ b/solution.py
@@ -43,14 +43,15 @@
     return value
 
 
-def kernel(order, ne, elements, s_ref, cnt_ref, w_ref, out_ref, pow_ref,
-           blocks, weights, rhs, part, first, second, counts,
+def kernel(order, ne, s_ref, flag_ref, w_ref, out_ref, pow_ref,
+           blocks, mask, weights, rhs, part, first, second, counts,
            ring_send, ring_recv, w_sem, s_sem, first_send, first_recv, second_send, second_recv,
-           cnt_send, cnt_recv, cnt_sem):
+           cnt_send, cnt_recv):
     nb = len(order)
     half = nb // 2
-    q, two_t, kq = s_ref.shape
-    tb = two_t // 2
+    _, tb, depth = s_ref.shape
+    q = PIECES
+    two_t, kq = 2 * tb, depth // q
     chunks, _, mo, width = part.shape
     group = width // two_t
     ways = ne // 2
@@ -69,16 +70,17 @@
     def slot_of(way, d):
         return d if (way == 0 or d in (0, half)) else half + d
 
-    arrivals = [[(d, j) for d in range(1, half) for j in range(q)]
-                + [(half, j) for j in (range(q // 2) if way == 0 else range(q // 2, q))]
-                for way in (0, 1)]
+    last = (((half - 1, 0), (half - 1, 1), (half, 0), (half - 1, 2), (half, 1), (half - 1, 3)),
+            ((half - 1, 2), (half - 1, 3), (half - 1, 0), (half, 2), (half - 1, 1), (half, 3)))
+    arrivals = [[(d, j) for d in range(1, half - 1) for j in range(q)]
+                + [(d, j) for d, j in last[way] if d > 0] for way in (0, 1)]
     number = [{item: k for k, item in enumerate(a)} for a in arrivals]
 
     def ring_copy(way, d, j):
         k = number[way][(d, j)]
         return pltpu.make_async_remote_copy(
-            src_ref=blocks.at[slot_of(way, d - 1), j],
-            dst_ref=blocks.at[slot_of(way, d), j],
+            src_ref=(s_ref if d == 1 else blocks.at[slot_of(way, d - 1)]).at[:, :, pl.ds(j * kq, kq)],
+            dst_ref=blocks.at[slot_of(way, d), :, :, pl.ds(j * kq, kq)],
             send_sem=ring_send.at[way, k], recv_sem=ring_recv.at[way, k],
             device_id={"beam": ahead if way == 0 else behind}, device_id_type=MESH)
 
@@ -88,7 +90,7 @@
 
     def count_copy(r):
         return pltpu.make_async_remote_copy(
-            src_ref=cnt_ref, dst_ref=counts.at[r], send_sem=cnt_send.at[r - 1], recv_sem=cnt_recv.at[r - 1],
+            src_ref=flag_ref, dst_ref=counts.at[r - 1], send_sem=cnt_send.at[r - 1], recv_sem=cnt_recv.at[r - 1],
             device_id={"elem": lax.rem(me_e + r, ne)}, device_id_type=MESH)
 
     def kept(i):
@@ -111,8 +113,6 @@
 
     own_in = pltpu.make_async_copy(s_ref, blocks.at[0], s_sem)
     own_in.start()
-    own_cnt = pltpu.make_async_copy(cnt_ref, counts.at[0], cnt_sem)
-    own_cnt.start()
 
     barrier = pltpu.get_barrier_semaphore()
     for b in (ahead, behind):
@@ -121,17 +121,28 @@
         pl.semaphore_signal(barrier, inc=1, device_id={"elem": lax.rem(me_e + r, ne)}, device_id_type=MESH)
     pl.semaphore_wait(barrier, 2 + ne - 1)
 
-    own_in.wait()
-    for j in range(q):
+    arrived = {((0, 0), j) for j in range(q)}
+    sent = [0, 0]
+
+    def send_ready():
         for way in (0, 1):
-            if (1, j) in number[way]:
-                ring_copy(way, 1, j).start()
+            while sent[way] < len(arrivals[way]):
+                d, j = arrivals[way][sent[way]]
+                if d > 1 and ((way, d - 1), j) not in arrived:
+                    break
+                ring_copy(way, d, j).start()
+                sent[way] += 1
+
+    send_ready()
     for r in range(1, ne):
         count_copy(r).start()
     for j in range(q):
         for i in (0, 1):
             weight_copy(i, j).start()
 
+    mask[...] = jnp.broadcast_to(flag_ref[...].astype(jnp.float32).astype(jnp.bfloat16), mask.shape)
+    own_in.wait()
+
     sequence = [(0, 0)]
     for d in range(1, half):
         sequence += [(0, d), (1, d)]
@@ -142,8 +153,9 @@
 
     def stage(c, j):
         for s, (way, d) in enumerate(members(c)):
-            re = blocks[slot_of(way, d), j, :tb, :]
-            im = blocks[slot_of(way, d), j, tb:, :]
+            columns = pl.ds(j * kq, kq)
+            re = blocks[slot_of(way, d), 0, :, columns] * mask[:, columns]
+            im = blocks[slot_of(way, d), 1, :, columns] * mask[:, columns]
             lo, hi = s * tb, (group + s) * tb
             rhs[lo:lo + tb, :kq] = re
             rhs[hi:hi + tb, :kq] = im
@@ -195,7 +207,6 @@
         if c < chunks - 1:
             waiting.append(c)
 
-    arrived = {((0, 0), j) for j in range(q)}
     todo = [(c, j) for c in range(chunks) for j in range(q)]
 
     def run_ready():
@@ -208,9 +219,8 @@
         for way in (0, 1):
             d, j = arrivals[way][k]
             ring_copy(way, d, j).wait_recv()
-            if (d + 1, j) in number[way]:
-                ring_copy(way, d + 1, j).start()
             arrived.add(((0 if d == half else way, d), j))
+            send_ready()
         for c in waiting:
             pass_on(c)
         waiting.clear()
@@ -219,12 +229,11 @@
         pass_on(c)
     waiting.clear()
 
-    own_cnt.wait()
-    total = counts[0]
+    live = flag_ref[...].astype(jnp.float32)
     for r in range(1, ne):
         count_copy(r).wait()
-        total = total + counts[r]
-    gain = jnp.sqrt(jnp.float32(elements) / total)[0:1, 0:1]
+        live = live + counts[r - 1].astype(jnp.float32)
+    gain = jnp.sqrt(jnp.float32(depth * ne) / jnp.sum(live, axis=1, keepdims=True))
 
     square = jnp.zeros((mo, width), jnp.float32)
     moved = jnp.zeros((mo, 2 * snaps), jnp.float32)
@@ -251,7 +260,7 @@
     out_ref[0] = moved[:, :snaps]
     out_ref[1] = moved[:, snaps:]
     power = jnp.sum(square, axis=1, keepdims=True) * (1.0 / snaps)
-    pow_ref[...] = jnp.broadcast_to(power, pow_ref.shape)
+    pow_ref[...] = jnp.broadcast_to(power, (mo, LANES)).T[0:1, :]
 
     for way in (0, 1):
         for d, j in arrivals[way]:
@@ -275,36 +284,34 @@
     width = 2 * group * tb
     ways = ne // 2
     items = q * (nb // 2) - q // 2
-    masked = signals * element_flags.astype(jnp.bfloat16)[None, :, None]
-    sent = masked.reshape(2, q, kq, tb).transpose(1, 0, 3, 2).reshape(q, 2 * tb, kq)
-    count = jnp.broadcast_to(jnp.sum(element_flags.astype(jnp.float32)), (8, LANES))
     dma = pltpu.SemaphoreType.DMA
     anywhere = pl.BlockSpec(memory_space=pl.ANY)
     vmem = pl.BlockSpec(memory_space=pltpu.VMEM)
     out, power = pl.pallas_call(
-        functools.partial(kernel, order, ne, depth * ne),
+        functools.partial(kernel, order, ne),
         out_shape=(jax.ShapeDtypeStruct((2, mo, nb * tb), jnp.bfloat16),
-                   jax.ShapeDtypeStruct((mo, LANES), jnp.float32)),
-        in_specs=[anywhere, anywhere, anywhere],
+                   jax.ShapeDtypeStruct((1, mo), jnp.float32)),
+        in_specs=[anywhere, vmem, anywhere],
         out_specs=(vmem, vmem),
         scratch_shapes=[
-            pltpu.VMEM((nb, q, 2 * tb, kq), jnp.bfloat16),
+            pltpu.VMEM((nb, 2, tb, depth), jnp.bfloat16),
+            pltpu.VMEM((tb, depth), jnp.bfloat16),
             pltpu.VMEM((q, rows, 2 * kq), jnp.bfloat16),
             pltpu.VMEM((width, 2 * kq), jnp.bfloat16),
             pltpu.VMEM((chunks, ne, mo, width), jnp.float32),
             pltpu.VMEM((chunks, ways, mo, width), jnp.float32),
             pltpu.VMEM((chunks, max(1, ways - 1), mo, width), jnp.float32),
-            pltpu.VMEM((ne, 8, LANES), jnp.float32),
+            pltpu.VMEM((ne - 1, 1, depth), jnp.int32),
             dma((2, items)), dma((2, items)), dma((2, q)), dma,
             dma((chunks, ways)), dma((chunks, ways)),
             dma((chunks, max(1, ways - 1))), dma((chunks, max(1, ways - 1))),
-            dma((ne - 1,)), dma((ne - 1,)), dma,
+            dma((ne - 1,)), dma((ne - 1,)),
         ],
         compiler_params=pltpu.CompilerParams(
             collective_id=0, has_side_effects=True, vmem_limit_bytes=60 * 2**20),
         name="beamform",
-    )(sent, count, weights)
-    return out, power[:, 0]
+    )(signals.transpose(0, 2, 1), element_flags.reshape(1, depth), weights)
+    return out, power.reshape(mo)
 
 
 def solution(mesh):

time: 80.8 us -> 72.2 us (0.89)
  other arithmetic: 3.13 us -> 0 us
  Pallas kernels: 71 us -> 68.2 us
  local copies, waits for them, and re-layouts: 5.61 us -> 3.12 us
    pallas_call x1, Pallas kernels: 71 us -> 68.2 us  [body(): pl.pallas_call(functools.partial(kernel, order, ne), out_shape=(jax.Shape...]
    slice x1 -> x0, local copies, waits for them, and re-layouts: 1.68 us -> none  [body(): return (out, power[:, 0])]
    reduce_sum x1 -> x0, other arithmetic: 1.33 us -> none  [body(): jnp.sum(element_flags.astype(jnp.float32))]
    unnamed x1 -> x2, local copies, waits for them, and re-layouts: 1.87 us -> 3.12 us
    broadcast_in_dim x1 -> x0, local copies, waits for them, and re-layouts: 1.23 us -> none  [body(): jnp.broadcast_to(jnp.sum(element_flags.astype(jnp.float32)), (8, LANES))]
    mul x1 -> x0, other arithmetic: 1.08 us -> none  [body(): masked = signals * element_flags.astype(jnp.bfloat16)[None, :, None]]
    reshape x1 -> x0, local copies, waits for them, and re-layouts: 0.84 us -> none  [body(): masked.reshape(2, q, kq, tb).transpose(1, 0, 3, 2).reshape(q, 2 * tb, kq)]
where the time goes in v2:
time: 72.2 us; the launch traced here: 71.9 us
  Pallas kernels  68.2 us (94%)
  local copies, waits for them, and re-layouts  3.12 us (4%)
    pallas_call x1, Pallas kernels, body(): pl.pallas_call(functools.partial(kernel, order, ne), out_shape=(jax.Shape...  68.2 us
    unnamed x2, local copies, waits for them, and re-layouts  3.12 us

profile of v2, /device:TPU:0, one launch (start us, length us, event | category | flops | bytes accessed | tf_op | source)
XLA Modules:
  0.0 71.9 jit_solution(13419104728691001070)
XLA Ops:
  0.6 68.2 %beamform.1 = (bf16[2,512,256]{2,1,0:T(8,128)(2,1)}, f32[1,512]{1,0:T(1,128)}) custom-call(bf16[2,32,4096]{2,1,0:T(8,128)(2,1)} %bitcast.3, s32[1,4096]{1,0:T(1,128)} %bitcast.4, bf16[2,2048,4096]{2,1,0:T(8,128)(2,1)} %w_ref.1), custom_call_target="tpu_custom_call" | custom-call | tf_op jit(solution)/shard_map/beamform/pallas_call | solution.py:290
  68.8 1.9 %copy.7 = bf16[2,512,256]{2,1,0:T(8,128)(2,1)} copy(bf16[2,512,256]{2,1,0:T(8,128)(2,1)} %get-tuple-element.8) | data formatting | bytes 1048576
  70.7 1.3 %copy.8 = f32[512]{0:T(512)} copy(f32[512]{0:T(512)} %bitcast.5) | data formatting | bytes 4096

commit v3 on v2

--- a/solution.py
+++ b/solution.py
@@ -9,6 +9,7 @@
 
 PIECES = 4
 LANES = 128
+SPLIT = 2
 MESH = pl.DeviceIdType.MESH
 
 
@@ -70,10 +71,16 @@
     def slot_of(way, d):
         return d if (way == 0 or d in (0, half)) else half + d
 
-    last = (((half - 1, 0), (half - 1, 1), (half, 0), (half - 1, 2), (half, 1), (half - 1, 3)),
-            ((half - 1, 2), (half - 1, 3), (half - 1, 0), (half, 2), (half - 1, 1), (half, 3)))
-    arrivals = [[(d, j) for d in range(1, half - 1) for j in range(q)]
-                + [(d, j) for d, j in last[way] if d > 0] for way in (0, 1)]
+    if half == 4:
+        arrivals = [[(1, 0), (1, 1), (2, 0), (1, 2), (2, 1), (1, 3), (2, 2), (2, 3),
+                     (3, 0), (3, 1), (3, 2), (3, 3), (4, 2), (4, 3)],
+                    [(1, 0), (1, 1), (2, 0), (1, 2), (3, 0), (1, 3), (2, 1), (4, 0),
+                     (3, 1), (2, 2), (4, 1), (2, 3), (3, 2), (3, 3)]]
+    else:
+        last = (((half - 1, 0), (half - 1, 1), (half - 1, 2), (half - 1, 3), (half, 2), (half, 3)),
+                ((half - 1, 0), (half - 1, 1), (half, 0), (half - 1, 2), (half, 1), (half - 1, 3)))
+        arrivals = [[(d, j) for d in range(1, half - 1) for j in range(q)]
+                    + [(d, j) for d, j in last[way] if d > 0] for way in (0, 1)]
     number = [{item: k for k, item in enumerate(a)} for a in arrivals]
 
     def ring_copy(way, d, j):
@@ -105,10 +112,18 @@
             send_sem=first_send.at[c, i], recv_sem=first_recv.at[c, i],
             device_id={"elem": partner}, device_id_type=MESH)
 
-    def second_copy(c, i):
+    def parts_of(c):
+        return SPLIT if c == chunks - 1 else 1
+
+    def rows_of(c, h):
+        size = mo // parts_of(c)
+        return slice(h * size, (h + 1) * size)
+
+    def second_copy(c, i, h):
+        rows = pl.ds(h * (mo // parts_of(c)), mo // parts_of(c))
         return pltpu.make_async_remote_copy(
-            src_ref=first.at[c, i], dst_ref=second.at[c, i - 1],
-            send_sem=second_send.at[c, i - 1], recv_sem=second_recv.at[c, i - 1],
+            src_ref=first.at[c, i, rows], dst_ref=second.at[c, i - 1, rows],
+            send_sem=second_send.at[c, i - 1, h], recv_sem=second_recv.at[c, i - 1, h],
             device_id={"elem": kept(i)}, device_id_type=MESH)
 
     own_in = pltpu.make_async_copy(s_ref, blocks.at[0], s_sem)
@@ -175,11 +190,12 @@
     weights_here = set()
     waiting = []
 
-    def pass_on(c):
-        for i in range(1, ways):
-            first_copy(c, i).wait_recv()
-            first[c, i] += part[c, kept(i)]
-            second_copy(c, i).start()
+    def pass_on(c, i):
+        first_copy(c, i).wait_recv()
+        for h in range(parts_of(c)):
+            rows = rows_of(c, h)
+            first[c, i, rows] += part[c, kept(i), rows]
+            second_copy(c, i, h).start()
 
     def piece(c, j):
         stage(c, j)
@@ -200,9 +216,7 @@
         for i in range(1, ways):
             multiply(c, j, kept(i), fresh)
             if c == chunks - 1:
-                first_copy(c, i).wait_recv()
-                first[c, i] += part[c, kept(i)]
-                second_copy(c, i).start()
+                pass_on(c, i)
         multiply(c, j, kept(0), fresh)
         if c < chunks - 1:
             waiting.append(c)
@@ -222,11 +236,13 @@
             arrived.add(((0 if d == half else way, d), j))
             send_ready()
         for c in waiting:
-            pass_on(c)
+            for i in range(1, ways):
+                pass_on(c, i)
         waiting.clear()
         run_ready()
     for c in waiting:
-        pass_on(c)
+        for i in range(1, ways):
+            pass_on(c, i)
     waiting.clear()
 
     live = flag_ref[...].astype(jnp.float32)
@@ -235,16 +251,7 @@
         live = live + counts[r - 1].astype(jnp.float32)
     gain = jnp.sqrt(jnp.float32(depth * ne) / jnp.sum(live, axis=1, keepdims=True))
 
-    square = jnp.zeros((mo, width), jnp.float32)
-    moved = jnp.zeros((mo, 2 * snaps), jnp.float32)
-    for c in range(chunks):
-        first_copy(c, 0).wait_recv()
-        value = part[c, me_e] + first[c, 0]
-        for i in range(1, ways):
-            second_copy(c, i).wait_recv()
-            value = value + second[c, i - 1]
-        value = value * gain
-        square = square + value * value
+    def selection(c):
         column = lax.broadcasted_iota(jnp.int32, (width, 2 * snaps), 0)
         target = lax.broadcasted_iota(jnp.int32, (width, 2 * snaps), 1)
         wanted = column
@@ -254,12 +261,35 @@
                 lo = (p * group + s) * tb
                 inside = (column >= lo) & (column < lo + tb)
                 wanted = jnp.where(inside, column - lo + p * snaps + source * tb, wanted)
-        select = jnp.where(wanted == target, 1.0, 0.0).astype(jnp.bfloat16)
-        moved = moved + jnp.dot(value.astype(jnp.bfloat16), select, preferred_element_type=jnp.float32)
-    moved = moved.astype(jnp.bfloat16)
-    out_ref[0] = moved[:, :snaps]
-    out_ref[1] = moved[:, snaps:]
-    power = jnp.sum(square, axis=1, keepdims=True) * (1.0 / snaps)
+        return jnp.where(wanted == target, 1.0, 0.0).astype(jnp.bfloat16)
+
+    def finished(c, h):
+        rows = rows_of(c, h)
+        value = part[c, me_e, rows] + first[c, 0, rows]
+        for i in range(1, ways):
+            second_copy(c, i, h).wait_recv()
+            value = value + second[c, i - 1, rows]
+        return value * gain
+
+    square = jnp.zeros((mo, width), jnp.float32)
+    moved = jnp.zeros((mo, 2 * snaps), jnp.float32)
+    for c in range(chunks - 1):
+        first_copy(c, 0).wait_recv()
+        value = finished(c, 0)
+        square = square + value * value
+        moved = moved + jnp.dot(value.astype(jnp.bfloat16), selection(c), preferred_element_type=jnp.float32)
+    c = chunks - 1
+    select = selection(c)
+    first_copy(c, 0).wait_recv()
+    squares = []
+    for h in range(SPLIT):
+        rows = rows_of(c, h)
+        value = finished(c, h)
+        squares.append(square[rows] + value * value)
+        all_moved = moved[rows] + jnp.dot(value.astype(jnp.bfloat16), select, preferred_element_type=jnp.float32)
+        out_ref[0, rows] = all_moved[:, :snaps].astype(jnp.bfloat16)
+        out_ref[1, rows] = all_moved[:, snaps:].astype(jnp.bfloat16)
+    power = jnp.concatenate([jnp.sum(v, axis=1, keepdims=True) for v in squares], axis=0) * (1.0 / snaps)
     pow_ref[...] = jnp.broadcast_to(power, (mo, LANES)).T[0:1, :]
 
     for way in (0, 1):
@@ -269,7 +299,8 @@
         for i in range(ways):
             first_copy(c, i).wait_send()
         for i in range(1, ways):
-            second_copy(c, i).wait_send()
+            for h in range(parts_of(c)):
+                second_copy(c, i, h).wait_send()
 
 
 def body(order, ne, signals, weights, element_flags):
@@ -285,7 +316,7 @@
     ways = ne // 2
     items = q * (nb // 2) - q // 2
     dma = pltpu.SemaphoreType.DMA
-    anywhere = pl.BlockSpec(memory_space=pl.ANY)
+    anywhere = pl.BlockSpec(memory_space=pltpu.MemorySpace.HBM)
     vmem = pl.BlockSpec(memory_space=pltpu.VMEM)
     out, power = pl.pallas_call(
         functools.partial(kernel, order, ne),
@@ -304,11 +335,11 @@
             pltpu.VMEM((ne - 1, 1, depth), jnp.int32),
             dma((2, items)), dma((2, items)), dma((2, q)), dma,
             dma((chunks, ways)), dma((chunks, ways)),
-            dma((chunks, max(1, ways - 1))), dma((chunks, max(1, ways - 1))),
+            dma((chunks, max(1, ways - 1), SPLIT)), dma((chunks, max(1, ways - 1), SPLIT)),
             dma((ne - 1,)), dma((ne - 1,)),
         ],
         compiler_params=pltpu.CompilerParams(
-            collective_id=0, has_side_effects=True, vmem_limit_bytes=60 * 2**20),
+            collective_id=0, has_side_effects=True, vmem_limit_bytes=50 * 2**20),
         name="beamform",
     )(signals.transpose(0, 2, 1), element_flags.reshape(1, depth), weights)
     return out, power.reshape(mo)

time: 72.2 us -> 67.9 us (0.940)
  Pallas kernels: 68.2 us -> 63.9 us
    pallas_call x1, Pallas kernels: 68.2 us -> 63.9 us  [body(): pl.pallas_call(functools.partial(kernel, order, ne), out_shape=(jax.Shape...]
    unnamed x2 -> x6, local copies, waits for them, and re-layouts: 3.12 us -> 3.13 us
where the time goes in v3:
time: 67.9 us; the launch traced here: 67.6 us
  Pallas kernels  63.9 us (94%)
  local copies, waits for them, and re-layouts  3.13 us (5%)
    pallas_call x1, Pallas kernels, body(): pl.pallas_call(functools.partial(kernel, order, ne), out_shape=(jax.Shape...  63.9 us
    unnamed x6, local copies, waits for them, and re-layouts  3.13 us

profile of v3, /device:TPU:0, one launch (start us, length us, event | category | flops | bytes accessed | tf_op | source)
XLA Modules:
  0.0 67.6 jit_solution(10056880764691397294)
XLA Ops:
  0.6 0.0 copy-start
  0.6 1.0 %copy-done = bf16[2,4096,32]{1,2,0:T(8,128)(2,1)S(1)} copy-done((bf16[2,4096,32]{1,2,0:T(8,128)(2,1)S(1)}, bf16[2,4096,32]{1,2,0:T(8,128)(2,1)}, u32[]{:S(2)}) %copy-start) | copy-done | bytes 524312
  1.7 0.0 copy-start.1
  1.7 0.7 %copy-done.1 = s32[4096]{0:T(1024)S(1)} copy-done((s32[4096]{0:T(1024)S(1)}, s32[4096]{0:T(1024)}, u32[]{:S(2)}) %copy-start.1) | copy-done | bytes 16408
  2.4 63.9 %beamform.1 = (bf16[2,512,256]{2,1,0:T(8,128)(2,1)S(1)}, f32[1,512]{1,0:T(1,128)S(1)}) custom-call(bf16[2,32,4096]{2,1,0:T(8,128)(2,1)S(1)} %bitcast.3, s32[1,4096]{1,0:T(1,128)S(1)} %bitcast.4, bf16[2,2048,4096]{2,1,0:T(8,128)(2,1)} %w_ref.1), custom_call_target="tpu_custom_call" | custom-call | tf_op jit(solution)/shard_map/beamform/pallas_call | solution.py:321
  66.3 0.8 %copy.7 = bf16[2,512,256]{2,1,0:T(8,128)(2,1)} copy(bf16[2,512,256]{2,1,0:T(8,128)(2,1)S(1)} %get-tuple-element.8) | data formatting | bytes 1048576
  67.1 0.6 copy.8
Async XLA Ops:
  0.6 1.0 %copy-start = (bf16[2,4096,32]{1,2,0:T(8,128)(2,1)S(1)}, bf16[2,4096,32]{1,2,0:T(8,128)(2,1)}, u32[]{:S(2)}) copy-start(bf16[2,4096,32]{1,2,0:T(8,128)(2,1)} %param.3) | copy-start | bytes 1572868
  1.7 0.7 %copy-start.1 = (s32[4096]{0:T(1024)S(1)}, s32[4096]{0:T(1024)}, u32[]{:S(2)}) copy-start(s32[4096]{0:T(1024)} %param.5) | copy-start | bytes 49156
